TPU v7x, 32 devices: a whole 2x2x4 slice. The times are simulated.
32 devices in a mesh: tp: 8 (over y, x, core), dp: 4 (over z).
Axes of the slice: x: 2, y: 2, z: 4, core: 2. Of those that a mesh axis runs over, the one named last changes fastest.
Arguments:
- grad_out: bfloat16 [1792, 8192], P(('dp', 'tp')), may hold values from -6 to 6
- gate_act: bfloat16 [1792, 14336], P('dp', 'tp'), may hold values from -8 to 8
- up_act: bfloat16 [1792, 14336], P('dp', 'tp'), may hold values from -6 to 6
- down_weight: bfloat16 [14336, 8192], P('tp'), may hold values from -0.0625 to 0.0625
Outputs:
- grad_gate: bfloat16 [1792, 14336], P('dp', 'tp')
- grad_up: bfloat16 [1792, 14336], P('dp', 'tp')
- grad_down: bfloat16 [14336, 8192], P(('tp', 'dp'))
All inputs are finite; a program needn't handle non-finite values.
Results may differ from a plain program's by a relative error of at most 0.013.
Values may be sent and summed in bfloat16 or wider, within the bound.
No kernel may reach another device: no remote copies, remote signals or barrier semaphores. Data moves between devices by JAX's collectives and lax.ppermute only.
A program may use at most 128 MiB of HBM per device.

v0:
```python
import math
import jax
import jax.numpy as jnp
from jax import lax
from jax.sharding import PartitionSpec as P


def body(grad_out, gate_act, up_act, down_weight):
    gate_val = gate_act.astype(jnp.float32)
    up_val = up_act.astype(jnp.float32)
    squash = jax.nn.sigmoid(gate_val)
    hidden = (gate_val * squash * up_val).astype(jnp.bfloat16)
    incoming = lax.all_gather(grad_out, "tp", axis=0, tiled=True)
    row_store = incoming
    new_rows = lax.dot_general(
        incoming, down_weight, (((1,), (1,)), ((), ())), preferred_element_type=jnp.float32
    )
    row_store, grad_hidden = (row_store, new_rows)
    weight_part = lax.dot_general(
        hidden, row_store, (((0,), (0,)), ((), ())), preferred_element_type=jnp.float32
    )
    summed = lax.psum_scatter(
        weight_part.astype(jnp.bfloat16), "dp", scatter_dimension=0, tiled=True
    ).astype(jnp.float32)
    grad_gate = (grad_hidden * up_val * squash * (1.0 + gate_val * (1.0 - squash))).astype(
        jnp.bfloat16
    )
    grad_up = (grad_hidden * gate_val * squash).astype(jnp.bfloat16)
    token_total = grad_out.shape[0] * lax.axis_size("tp") * lax.axis_size("dp")
    grad_scale = 1.0 / math.sqrt(token_total)
    grad_down = (summed * grad_scale).astype(jnp.bfloat16)
    return (grad_gate, grad_up, grad_down)


def solution(mesh):
    return jax.shard_map(
        body,
        mesh=mesh,
        in_specs=(P(("dp", "tp"), None), P("dp", "tp"), P("dp", "tp"), P("tp", None)),
        out_specs=(P("dp", "tp"), P("dp", "tp"), P(("tp", "dp"), None)),
        check_vma=False,
    )
```

profile of v0, /device:TPU:16, one launch (start us, length us, event | category | flops | bytes accessed | tf_op | source)
XLA Modules:
  0.0 582.6 jit_solution(4607834574746264727)
XLA Ops:
  7.2 0.0 all-gather.2.cloned.1.call-start
  7.2 0.7 all-gather.2.cloned.1.call-update
  7.9 0.0 reduce-scatter.2.cloned.1.call-start
  7.9 52.8 %all-gather.2.cloned.1.call-done = bf16[448,8192]{1,0:T(8,128)(2,1)} async-done(((bf16[56,8192]{1,0:T(8,128)(2,1)}), bf16[448,8192]{1,0:T(8,128)(2,1)}) %all-gather.2.cloned.1.call-update) | async-done | bytes 7340048 | tf_op jit(solution)/shard_map/all_gather | solution.py:13
  60.8 23.1 %convolution_convert_fusion = bf16[1792,8192]{1,0:T(8,128)(2,1)} fusion(bf16[448,8192]{1,0:T(8,128)(2,1)} %all-gather.2.cloned.1.call-done, bf16[448,1792]{1,0:T(8,128)(2,1)} %param.6, bf16[448,1792]{1,0:T(8,128)(2,1)} %param.5), kind=kOutput, calls=%fused_computation | convolution fusion | flops 13174439936 | bytes 39911424 | tf_op jit(solution)/shard_map/dot_general | solution.py:19
  83.9 0.0 copy-start
  83.9 0.0 copy-start.1
  83.9 0.0 reduce-scatter.2.cloned.1.call-update
  83.9 1.4 copy-done
  85.3 0.5 copy-done.1
  85.8 26.9 %fusion.9 = (bf16[448,1792]{1,0:T(8,128)(2,1)}, bf16[448,1792]{1,0:T(8,128)(2,1)}) fusion(bf16[448,1792]{1,0:T(8,128)(2,1)S(1)} %copy-done, bf16[448,1792]{1,0:T(8,128)(2,1)S(1)} %copy-done.1, bf16[448,8192]{1,0:T(8,128)(2,1)} %all-gather.2.cloned.1.call-done, bf16[1792,8192]{1,0:T(8,128)(2,1)} %param.7), kind=kOutput, calls=%fused_computation.17 | convolution fusion | flops 13165379584 | bytes 43122688 | tf_op jit(solution)/shard_map/dot_general | solution.py:15
  112.7 455.1 %reduce-scatter.2.cloned.1.call-done = bf16[448,8192]{1,0:T(8,128)(2,1)} async-done(((bf16[1792,8192]{1,0:T(8,128)(2,1)}), bf16[448,8192]{1,0:T(8,128)(2,1)}) %reduce-scatter.2.cloned.1.call-update) | async-done | bytes 7340048 | tf_op jit(solution)/shard_map/reduce_scatter | solution.py:22
  567.8 7.9 %multiply_convert_fusion = bf16[448,8192]{1,0:T(8,128)(2,1)} fusion(bf16[448,8192]{1,0:T(8,128)(2,1)} %reduce-scatter.2.cloned.1.call-done), kind=kLoop, calls=%fused_computation.1 | loop fusion | flops 11010048 | bytes 14680064 | tf_op jit(solution)/shard_map/convert_element_type | solution.py:31
Async XLA Ops:
  7.2 53.6 %all-gather.2.cloned.1.call-start = ((), (), s32[]{:S(2)}) async-start(), calls=%async_computation.1 | async-start | bytes 8257536 | tf_op jit(solution)/shard_map/all_gather | solution.py:13
  7.9 559.9 %reduce-scatter.2.cloned.1.call-start = ((), (), s32[]{:S(2)}) async-start(), calls=%async_computation.2 | async-start | bytes 36700160 | tf_op jit(solution)/shard_map/reduce_scatter | solution.py:22
  83.9 1.4 copy-start
  83.9 1.9 copy-start.1
Sparse Core Ops, SparseCore 0:
  9.9 50.8 all-gather.1
  84.0 483.7 reduce-scatter.1
where the time goes:
time: 583 us
  waiting for transfers between devices  509 us (87%)
  matrix products  50 us (9%)
  between operations  14 us (2%)
  other arithmetic  7.93 us (1%)
    reduce_scatter x1, waiting for transfers between devices, body(): lax.psum_scatter(weight_part.astype(jnp.bfloat16), 'dp', scatter_dimensio...  455 us
    all_gather x1, waiting for transfers between devices, body(): incoming = lax.all_gather(grad_out, 'tp', axis=0, tiled=True)  52.8 us
    dot_general x1, matrix products, body(): lax.dot_general(incoming, down_weight, (((1,), (1,)), ((), ())), preferre...  26.9 us
    dot_general x1, matrix products, body(): lax.dot_general(hidden, row_store, (((0,), (0,)), ((), ())), preferred_el...  23.1 us
  transfers between devices with their start and end apart: 2, of which 2 were waited for; matrix products, arithmetic and copies ran while one was open for 5% of the time, Pallas kernels for 0%

commit v1 on v0

--- a/solution.py
+++ b/solution.py
@@ -10,7 +10,11 @@
     up_val = up_act.astype(jnp.float32)
     squash = jax.nn.sigmoid(gate_val)
     hidden = (gate_val * squash * up_val).astype(jnp.bfloat16)
-    incoming = lax.all_gather(grad_out, "tp", axis=0, tiled=True)
+    draw_goods = lambda a_name, mine_x: jnp.concatenate(
+        lax.all_to_all(jnp.stack([mine_x for _ in range(lax.axis_size(a_name))]), a_name, 0, 0),
+        axis=0,
+    )
+    incoming = draw_goods("tp", grad_out)
     row_store = incoming
     new_rows = lax.dot_general(
         incoming, down_weight, (((1,), (1,)), ((), ())), preferred_element_type=jnp.float32

time: 583 us -> 616 us (1.057)
  blocking collectives: 0 us -> 86.6 us
  waiting for transfers between devices: 509 us -> 457 us
    all_to_all x0 -> x1, blocking collectives: none -> 86.6 us  [body(): lax.all_to_all(jnp.stack([mine_x for _ in range(lax.axis_size(a_name))]),...]
    all_gather x1 -> x0, waiting for transfers between devices: 52.8 us -> none  [body(): incoming = lax.all_gather(grad_out, 'tp', axis=0, tiled=True)]
  transfers between devices with their start and end apart: 2 -> 1, of which waited for: 2 -> 1; matrix products, arithmetic and copies ran while one was open for 5% -> 4% of each run, Pallas kernels for 0% -> 0%
where the time goes in v1:
time: 616 us
  waiting for transfers between devices  457 us (74%)
  blocking collectives  86.6 us (14%)
  matrix products  48.2 us (8%)
  between operations  14.1 us (2%)
  other arithmetic  7.93 us (1%)
    reduce_scatter x1, waiting for transfers between devices, body(): lax.psum_scatter(weight_part.astype(jnp.bfloat16), 'dp', scatter_dimensio...  457 us
    all_to_all x1, blocking collectives, body(): lax.all_to_all(jnp.stack([mine_x for _ in range(lax.axis_size(a_name))]),...  86.6 us
    dot_general x1, matrix products, body(): lax.dot_general(incoming, down_weight, (((1,), (1,)), ((), ())), preferre...  26.1 us
    dot_general x1, matrix products, body(): lax.dot_general(hidden, row_store, (((0,), (0,)), ((), ())), preferred_el...  22.2 us
  transfers between devices with their start and end apart: 1, of which 1 were waited for; matrix products, arithmetic and copies ran while one was open for 4% of the time, Pallas kernels for 0%

profile of v1, /device:TPU:16, one launch (start us, length us, event | category | flops | bytes accessed | tf_op | source)
XLA Modules:
  0.0 616.0 jit_solution(665777458552893055)
XLA Ops:
  7.2 0.0 reduce-scatter.2.cloned.1.call-start
  7.2 2.0 stack.2
  9.3 0.0 copy-start
  9.3 0.0 copy-start.1
  9.3 86.6 %all_to_all.5 = bf16[8,56,8192]{2,1,0:T(8,128)(2,1)} all-to-all(bf16[8,56,8192]{2,1,0:T(8,128)(2,1)S(1)} %stack.2), channel_id=1, replica_groups=mesh['tp'=8,'dp'=4] {'tp'}, dimensions={0} | all-to-all | bytes 14680064 | tf_op jit(solution)/shard_map/all_to_all | solution.py:14
  95.9 0.0 copy-done
  95.9 0.0 copy-done.1
  95.9 22.2 %convolution_convert_fusion = bf16[1792,8192]{1,0:T(8,128)(2,1)} fusion(bf16[448,8192]{1,0:T(8,128)(2,1)} %bitcast.4, bf16[448,1792]{1,0:T(8,128)(2,1)S(1)} %copy-done.1, bf16[448,1792]{1,0:T(8,128)(2,1)S(1)} %copy-done), kind=kOutput, calls=%fused_computation | convolution fusion | flops 13174439936 | bytes 39911424 | tf_op jit(solution)/shard_map/dot_general | solution.py:23
  118.1 0.0 reduce-scatter.2.cloned.1.call-update
  118.1 26.1 %fusion.9 = (bf16[448,1792]{1,0:T(8,128)(2,1)}, bf16[448,1792]{1,0:T(8,128)(2,1)}) fusion(bf16[448,1792]{1,0:T(8,128)(2,1)S(1)} %copy-done, bf16[448,1792]{1,0:T(8,128)(2,1)S(1)} %copy-done.1, bf16[448,8192]{1,0:T(8,128)(2,1)} %bitcast.5, bf16[1792,8192]{1,0:T(8,128)(2,1)} %param.7), kind=kOutput, calls=%fused_computation.17 | convolution fusion | flops 13165379584 | bytes 43122688 | tf_op jit(solution)/shard_map/dot_general | solution.py:19
  144.2 457.1 %reduce-scatter.2.cloned.1.call-done = bf16[448,8192]{1,0:T(8,128)(2,1)} async-done(((bf16[1792,8192]{1,0:T(8,128)(2,1)}), bf16[448,8192]{1,0:T(8,128)(2,1)}) %reduce-scatter.2.cloned.1.call-update) | async-done | bytes 7340048 | tf_op jit(solution)/shard_map/reduce_scatter | solution.py:26
  601.2 7.9 %multiply_convert_fusion = bf16[448,8192]{1,0:T(8,128)(2,1)} fusion(bf16[448,8192]{1,0:T(8,128)(2,1)} %reduce-scatter.2.cloned.1.call-done), kind=kLoop, calls=%fused_computation.1 | loop fusion | flops 11010048 | bytes 14680064 | tf_op jit(solution)/shard_map/convert_element_type | solution.py:35
Async XLA Ops:
  7.2 594.1 %reduce-scatter.2.cloned.1.call-start = ((), (), s32[]{:S(2)}) async-start(), calls=%async_computation.2 | async-start | bytes 36700160 | tf_op jit(solution)/shard_map/reduce_scatter | solution.py:26
  9.3 86.7 %copy-start = (bf16[448,1792]{1,0:T(8,128)(2,1)S(1)}, bf16[448,1792]{1,0:T(8,128)(2,1)}, u32[]{:S(2)}) copy-start(bf16[448,1792]{1,0:T(8,128)(2,1)} %param.5) | copy-start | bytes 4816900
  9.3 86.6 %copy-start.1 = (bf16[448,1792]{1,0:T(8,128)(2,1)S(1)}, bf16[448,1792]{1,0:T(8,128)(2,1)}, u32[]{:S(2)}) copy-start(bf16[448,1792]{1,0:T(8,128)(2,1)} %param.6) | copy-start | bytes 4816900
Sparse Core Ops, SparseCore 0:
  118.2 482.9 reduce-scatter.1
